TPU v7x, 512 devices: a whole 4x8x8 slice. The times are simulated.
512 devices in a mesh: gx: 8 (over x, core), gy: 8 (over z), gz: 8 (over y).
Axes of the slice: x: 4, y: 8, z: 8, core: 2. Of those that a mesh axis runs over, the one named last changes fastest.
Arguments:
- outcomes: bfloat16 [393216, 2048], P(('gx', 'gy', 'gz')), may hold values from -6 to 6
- sketch: bfloat16 [393216, 128], P(('gx', 'gy', 'gz')), may hold values from -6 to 6
Outputs:
- left_basis: float32 [393216, 128], P(('gx', 'gy', 'gz'))
- factor: float32 [128, 128], replicated
All inputs are finite; a program needn't handle non-finite values.
Results may differ from a plain program's by a relative error of at most 0.005.
Values may be sent and summed in bfloat16 or wider, within the bound.
No kernel may reach another device: no remote copies, remote signals or barrier semaphores. Data moves between devices by JAX's collectives and lax.ppermute only.
A program may use at most 64 MiB of HBM per device.

v0:
```python
import math

import jax
import jax.numpy as jnp
from jax import lax
from jax.sharding import Mesh
from jax.sharding import PartitionSpec as P

POWER = 2
GX_GY_GZ = ("gx_0", "gx_1", "gy", "gz")


def in_blocks(shard, dim, length):
    before, after = (shard.shape[:dim], shard.shape[dim + 1 :])
    return jnp.moveaxis(shard.reshape(*before, length, -1, *after), dim, 0)


def summed_on_arrival(shard, axis, dim):
    length = lax.axis_size(axis)
    blocks = lax.all_to_all(in_blocks(shard, dim, length), axis, 0, 0, tiled=True)
    return jnp.sum(blocks, axis=0)


def sum_in_two_steps(shard, axes, dim):
    far, near = axes
    blocks = in_blocks(shard, dim, lax.axis_size(far))
    nearer = summed_on_arrival(blocks, near, dim + 1)
    arrived = lax.all_to_all(nearer, far, split_axis=0, concat_axis=0, tiled=True)
    return arrived.sum(axis=0)


def rows_for(lines, length):
    spare = -len(lines) % length
    return jnp.pad(lines, [(0, spare)] + [(0, 0)] * (lines.ndim - 1))


def sent_to_all(shard, axis):
    copies = jnp.broadcast_to(shard, (lax.axis_size(axis), *shard.shape))
    return lax.all_to_all(copies, axis, split_axis=0, concat_axis=0, tiled=True)


def in_order(blocks, dim):
    blocks = jnp.moveaxis(blocks, 0, dim)
    shape = blocks.shape
    return blocks.reshape(*shape[:dim], shape[dim] * shape[dim + 1], *shape[dim + 2 :])


def gathered_by_axis(shard, axes, dim):
    far, near = axes
    initial = sent_to_all(shard, far)
    blocks = jnp.swapaxes(sent_to_all(initial, near), 0, 1)
    return in_order(blocks.reshape(-1, *shard.shape), dim)


def total_of(shard, axes):
    lines = shard.reshape(-1, shard.shape[-1])
    own = sum_in_two_steps(
        rows_for(lines, lax.axis_size(axes[0]) * lax.axis_size(axes[1])), axes, 0
    )
    whole = gathered_by_axis(own, axes, 0)
    return whole[: len(lines)].reshape(shard.shape)


def sum_by_parts(shard, axes):
    lines = shard.reshape(-1)
    own = sum_in_two_steps(
        rows_for(lines, lax.axis_size(axes[0]) * lax.axis_size(axes[1])), axes, 0
    )
    whole = gathered_by_axis(own, axes, 0)
    return whole[: len(lines)].reshape(shard.shape)


def per_device(outcomes, sketch):
    device_count = lax.axis_size(GX_GY_GZ)
    rows_here = outcomes.shape[0]
    day_count = outcomes.shape[1]
    unit_count = rows_here * device_count
    current = sketch
    left_basis = None
    lower_tri = None
    for power_step in range(POWER):
        partial_sum = lax.dot_general(
            outcomes, current, (((0,), (0,)), ((), ())), preferred_element_type=jnp.float32
        )
        summed = total_of(partial_sum, (("gx_0", "gx_1"), ("gy", "gz")))
        day_weights = (summed / math.sqrt(unit_count)).astype(jnp.bfloat16)
        projected = jnp.dot(outcomes, day_weights, preferred_element_type=jnp.float32)
        projected = projected / math.sqrt(day_count)
        gram_local = jnp.dot(projected.T, projected, precision=lax.Precision.HIGHEST) / unit_count
        gram = sum_by_parts(gram_local, (("gx_0", "gx_1"), ("gy", "gz")))
        lower_tri = jnp.linalg.cholesky(gram)
        left_basis = lax.linalg.triangular_solve(
            lower_tri, projected, left_side=False, lower=True, transpose_a=True
        )
        current = left_basis.astype(jnp.bfloat16)
    return (left_basis, lower_tri.T)


def solution(mesh):
    finer = Mesh(
        mesh.devices.reshape(4, 2, mesh.shape["gy"], mesh.shape["gz"]), ("gx_0", "gx_1", "gy", "gz")
    )
    return jax.shard_map(
        per_device,
        mesh=finer,
        in_specs=(P(GX_GY_GZ, None), P(GX_GY_GZ, None)),
        out_specs=(P(GX_GY_GZ, None), P()),
        check_vma=False,
    )
```

profile of v0, /device:TPU:1, one launch (start us, length us, event | category | flops | bytes accessed | tf_op | source)
XLA Modules:
  0.0 415.9 jit_solution(5203106886307186492)
XLA Ops:
  4.8 44.5 %all_to_all.96 = f32[64,8,4,128]{3,2,1,0:T(4,128)} all-to-all(f32[64,8,4,128]{3,2,1,0:T(4,128)S(1)} %bitcast.68), channel_id=1, replica_groups=mesh['gx_0'=4,'gx_1'=2,'gy'=8,'gz'=8] {'gy','gz'}, dimensions={0} | all-to-all | bytes 2097152 | tf_op jit(solution)/shard_map/all_to_all | solution.py:20
  50.6 12.0 %all_to_all.97 = f32[8,4,128]{2,1,0:T(4,128)S(1)} all-to-all(f32[8,4,128]{2,1,0:T(4,128)S(1)} %reduce_sum.72), channel_id=1, replica_groups=mesh['gx_0'=4,'gx_1'=2,'gy'=8,'gz'=8] {'gx_0','gx_1'}, dimensions={0} | all-to-all | bytes 32768 | tf_op jit(solution)/shard_map/all_to_all | solution.py:28
  62.7 7.7 %all_to_all.98 = f32[8,4,128]{2,1,0:T(4,128)S(1)} all-to-all(f32[8,4,128]{2,1,0:T(4,128)S(1)} %broadcast_in_dim.25), channel_id=1, replica_groups=mesh['gx_0'=4,'gx_1'=2,'gy'=8,'gz'=8] {'gx_0','gx_1'}, dimensions={0} | all-to-all | bytes 32768 | tf_op jit(solution)/shard_map/all_to_all | solution.py:39
  70.7 33.4 %all_to_all.99 = f32[64,8,4,128]{3,2,1,0:T(4,128)S(1)} all-to-all(f32[64,8,4,128]{3,2,1,0:T(4,128)S(1)} %broadcast_in_dim.26), channel_id=1, replica_groups=mesh['gx_0'=4,'gx_1'=2,'gy'=8,'gz'=8] {'gy','gz'}, dimensions={0} | all-to-all | bytes 2097152 | tf_op jit(solution)/shard_map/all_to_all | solution.py:39
  112.0 18.9 %all_to_all.100 = f32[64,1,256]{2,1,0:T(1,128)} all-to-all(f32[64,1,256]{2,1,0:T(1,128)} %reshape.43), channel_id=1, replica_groups=mesh['gx_0'=4,'gx_1'=2,'gy'=8,'gz'=8] {'gy','gz'}, dimensions={0} | all-to-all | bytes 131072 | tf_op jit(solution)/shard_map/all_to_all | solution.py:20
  136.4 10.1 %all_to_all.101 = f32[8,1,32]{2,1,0:T(1,128)S(1)} all-to-all(f32[8,1,32]{2,1,0:T(1,128)S(1)} %bitcast.76), channel_id=1, replica_groups=mesh['gx_0'=4,'gx_1'=2,'gy'=8,'gz'=8] {'gx_0','gx_1'}, dimensions={0} | all-to-all | bytes 2048 | tf_op jit(solution)/shard_map/all_to_all | solution.py:28
  146.5 7.6 %all_to_all.102 = f32[8,1,32]{2,1,0:T(1,128)S(1)} all-to-all(f32[8,1,32]{2,1,0:T(1,128)S(1)} %broadcast_in_dim.27), channel_id=1, replica_groups=mesh['gx_0'=4,'gx_1'=2,'gy'=8,'gz'=8] {'gx_0','gx_1'}, dimensions={0} | all-to-all | bytes 2048 | tf_op jit(solution)/shard_map/all_to_all | solution.py:39
  156.6 16.5 %all_to_all.103 = f32[64,1,256]{2,1,0:T(1,128)} all-to-all(f32[64,1,256]{2,1,0:T(1,128)} %reshape.45), channel_id=1, replica_groups=mesh['gx_0'=4,'gx_1'=2,'gy'=8,'gz'=8] {'gy','gz'}, dimensions={0} | all-to-all | bytes 131072 | tf_op jit(solution)/shard_map/all_to_all | solution.py:39
  173.1 2.2 reduce.7
  183.4 13.2 %cholesky.44 = f32[128,128]{1,0:T(8,128)} custom-call(f32[128,128]{1,0:T(8,128)} %fusion.9), custom_call_target="Cholesky" | custom-call | tf_op jit(solution)/shard_map/jit(cholesky)/cholesky | solution.py:91
  200.2 11.3 %custom-call.6 = f32[1,128,128]{1,2,0:T(8,128)} custom-call(f32[1,128,128]{2,1,0:T(8,128)} %fusion.5), custom_call_target="InvertDiagBlocksLowerTriangular" | custom-call | tf_op jit(solution)/shard_map/triangular_solve/custom-call.0 | solution.py:92
  214.5 2.6 copy.45
  218.6 30.3 %all_to_all.104 = f32[64,8,4,128]{3,2,1,0:T(4,128)} all-to-all(f32[64,8,4,128]{3,2,1,0:T(4,128)S(1)} %copy.46), channel_id=1, replica_groups=mesh['gx_0'=4,'gx_1'=2,'gy'=8,'gz'=8] {'gy','gz'}, dimensions={0} | all-to-all | bytes 2097152 | tf_op jit(solution)/shard_map/all_to_all | solution.py:20
  250.3 12.0 %all_to_all.105 = f32[8,4,128]{2,1,0:T(4,128)S(1)} all-to-all(f32[8,4,128]{2,1,0:T(4,128)S(1)} %reduce_sum.76), channel_id=1, replica_groups=mesh['gx_0'=4,'gx_1'=2,'gy'=8,'gz'=8] {'gx_0','gx_1'}, dimensions={0} | all-to-all | bytes 32768 | tf_op jit(solution)/shard_map/all_to_all | solution.py:28
  262.3 7.7 %all_to_all.106 = f32[8,4,128]{2,1,0:T(4,128)S(1)} all-to-all(f32[8,4,128]{2,1,0:T(4,128)S(1)} %broadcast_in_dim.29), channel_id=1, replica_groups=mesh['gx_0'=4,'gx_1'=2,'gy'=8,'gz'=8] {'gx_0','gx_1'}, dimensions={0} | all-to-all | bytes 32768 | tf_op jit(solution)/shard_map/all_to_all | solution.py:39
  270.3 33.2 %all_to_all.107 = f32[64,8,4,128]{3,2,1,0:T(4,128)S(1)} all-to-all(f32[64,8,4,128]{3,2,1,0:T(4,128)S(1)} %broadcast_in_dim.30), channel_id=1, replica_groups=mesh['gx_0'=4,'gx_1'=2,'gy'=8,'gz'=8] {'gy','gz'}, dimensions={0} | all-to-all | bytes 2097152 | tf_op jit(solution)/shard_map/all_to_all | solution.py:39
  311.4 18.9 %all_to_all.108 = f32[64,1,256]{2,1,0:T(1,128)} all-to-all(f32[64,1,256]{2,1,0:T(1,128)} %reshape.47), channel_id=1, replica_groups=mesh['gx_0'=4,'gx_1'=2,'gy'=8,'gz'=8] {'gy','gz'}, dimensions={0} | all-to-all | bytes 131072 | tf_op jit(solution)/shard_map/all_to_all | solution.py:20
  330.3 2.2 reduce.8
  335.2 10.1 %all_to_all.109 = f32[8,1,32]{2,1,0:T(1,128)S(1)} all-to-all(f32[8,1,32]{2,1,0:T(1,128)S(1)} %bitcast.78), channel_id=1, replica_groups=mesh['gx_0'=4,'gx_1'=2,'gy'=8,'gz'=8] {'gx_0','gx_1'}, dimensions={0} | all-to-all | bytes 2048 | tf_op jit(solution)/shard_map/all_to_all | solution.py:28
  345.3 7.6 %all_to_all.110 = f32[8,1,32]{2,1,0:T(1,128)S(1)} all-to-all(f32[8,1,32]{2,1,0:T(1,128)S(1)} %broadcast_in_dim.31), channel_id=1, replica_groups=mesh['gx_0'=4,'gx_1'=2,'gy'=8,'gz'=8] {'gx_0','gx_1'}, dimensions={0} | all-to-all | bytes 2048 | tf_op jit(solution)/shard_map/all_to_all | solution.py:39
  355.4 16.5 %all_to_all.111 = f32[64,1,256]{2,1,0:T(1,128)} all-to-all(f32[64,1,256]{2,1,0:T(1,128)} %reshape.49), channel_id=1, replica_groups=mesh['gx_0'=4,'gx_1'=2,'gy'=8,'gz'=8] {'gy','gz'}, dimensions={0} | all-to-all | bytes 131072 | tf_op jit(solution)/shard_map/all_to_all | solution.py:39
  371.9 2.2 reduce.9
  382.3 13.2 %cholesky.55 = f32[128,128]{1,0:T(8,128)} custom-call(f32[128,128]{1,0:T(8,128)} %fusion.7), custom_call_target="Cholesky" | custom-call | tf_op jit(solution)/shard_map/jit(cholesky)/cholesky | solution.py:91
  400.7 11.3 %custom-call.7 = f32[1,128,128]{1,2,0:T(8,128)} custom-call(f32[1,128,128]{2,1,0:T(8,128)} %get-tuple-element.15), custom_call_target="InvertDiagBlocksLowerTriangular" | custom-call | tf_op jit(solution)/shard_map/triangular_solve/custom-call.0 | solution.py:92
  (62 shorter events, 70.0 us)
Async XLA Ops:
  0.6 1.9 copy-start
where the time goes:
time: 419 us; the launch traced here: 416 us
  blocking collectives  287 us (68%)
  other arithmetic  73.7 us (18%)
  local copies, waits for them, and re-layouts  43 us (10%)
  matrix products  11.5 us (3%)
    all_to_all x8, blocking collectives, sent_to_all(): return lax.all_to_all(copies, axis, split_axis=0, concat_axis=0, tiled=True)  130 us
    all_to_all x4, blocking collectives, summed_on_arrival(): lax.all_to_all(in_blocks(shard, dim, length), axis, 0, 0, tiled=True)  113 us
    all_to_all x4, blocking collectives, sum_in_two_steps(): lax.all_to_all(nearer, far, split_axis=0, concat_axis=0, tiled=True)  44.2 us
    another operation x6, other arithmetic, per_device(): lower_tri = jnp.linalg.cholesky(gram)  29.4 us
    another operation x3, other arithmetic, per_device(): lax.linalg.triangular_solve(lower_tri, projected, left_side=False, lower=...  24.7 us
    unnamed x12, local copies, waits for them, and re-layouts  19 us

commit v1 on v0

v1 whole, which is shorter than its diff:
```python
import math

import jax
import jax.numpy as jnp
from jax import lax
from jax.sharding import Mesh
from jax.sharding import PartitionSpec as P

X, C, Z, Y = "gx_0", "gx_1", "gy", "gz"
EVERY = (X, C, Z, Y)
F32, BF16 = jnp.float32, jnp.bfloat16
HIGHEST = lax.Precision.HIGHEST


def swap(block):
    return lax.ppermute(block, C, [(0, 1), (1, 0)])


def exchange(blocks, axes):
    return lax.all_to_all(blocks, axes, split_axis=0, concat_axis=0, tiled=True)


def to_all(block, axes):
    copies = jnp.broadcast_to(block, (lax.axis_size(axes), *block.shape))
    return exchange(copies, axes)


def own_half(whole):
    half = whole.shape[0] // 2
    core = lax.axis_index(C)
    mine = lax.dynamic_slice_in_dim(whole, core * half, half, 0)
    other = lax.dynamic_slice_in_dim(whole, (1 - core) * half, half, 0)
    return mine + swap(other)


def both_halves(mine):
    other = swap(mine)
    first = lax.axis_index(C) == 0
    return jnp.concatenate([jnp.where(first, mine, other), jnp.where(first, other, mine)], 0)


def scattered_sum(part, axes):
    blocks = part.reshape(lax.axis_size(axes), -1, part.shape[-1])
    return exchange(blocks, axes).sum(axis=0)


def gathered(own, axes):
    return to_all(own, axes).reshape(-1, own.shape[-1])


def row_sums(part):
    mine = own_half(part)
    mine = scattered_sum(mine, X)
    return scattered_sum(mine, (Z, Y))


def gram_sum(part):
    mine = scattered_sum(own_half(part), X)
    mine = to_all(mine, Z).sum(axis=0)
    mine = to_all(mine, Y).sum(axis=0)
    return both_halves(gathered(mine, X))


def transposed_dot(rows, columns):
    return lax.dot_general(rows, columns, (((0,), (0,)), ((), ())), preferred_element_type=F32)


def solved(lower, rows):
    return lax.linalg.triangular_solve(lower, rows, left_side=False, lower=True, transpose_a=True)


def per_device(outcomes, sketch):
    rows_here, day_count = outcomes.shape
    rank = sketch.shape[1]
    unit_count = rows_here * lax.axis_size(EVERY)
    per_unit, per_day = 1 / math.sqrt(unit_count), 1 / math.sqrt(day_count)

    own = row_sums(transposed_dot(outcomes, sketch))
    weights = both_halves(gathered((own * per_unit).astype(BF16), (X, Z, Y)))

    projected = jnp.dot(outcomes, weights, preferred_element_type=F32) * per_day
    high = projected.astype(BF16)
    low = (projected - high.astype(F32)).astype(BF16)
    split = transposed_dot(outcomes, jnp.concatenate([high, low], 1))
    own = row_sums(split[:, :rank] + split[:, rank:])
    back = both_halves(gathered(gathered(own, (Z, Y)), X))
    gram = lax.dot_general(
        weights.astype(F32), back, (((0,), (0,)), ((), ())), precision=HIGHEST
    ) * (per_day / unit_count)
    lower = jnp.linalg.cholesky(gram)
    weights = (solved(lower, back) * per_unit).astype(BF16)

    projected = jnp.dot(outcomes, weights, preferred_element_type=F32) * per_day
    gram = gram_sum(jnp.dot(projected.T, projected, precision=HIGHEST) / unit_count)
    lower = jnp.linalg.cholesky(gram)
    return solved(lower, projected), lower.T


def solution(mesh):
    finer = Mesh(
        mesh.devices.reshape(4, 2, mesh.shape["gy"], mesh.shape["gz"]), EVERY
    )
    return jax.shard_map(
        per_device,
        mesh=finer,
        in_specs=(P(EVERY, None), P(EVERY, None)),
        out_specs=(P(EVERY, None), P()),
        check_vma=False,
    )
```

time: 419 us -> 279 us (0.67)
  blocking collectives: 287 us -> 145 us
  starting transfers between devices: 0 us -> 33.4 us
  local copies, waits for them, and re-layouts: 43 us -> 12.5 us
  other arithmetic: 73.7 us -> 65.1 us
  waiting for transfers between devices: 0 us -> 8.35 us
    all_to_all x16 -> x11, blocking collectives: 287 us -> 145 us  [exchange(): return lax.all_to_all(blocks, axes, split_axis=0, concat_axis=0, tiled=True)]
    ppermute x0 -> x6, starting transfers between devices: none -> 33.4 us  [swap(): return lax.ppermute(block, C, [(0, 1), (1, 0)])]
    unnamed x12 -> x19, local copies, waits for them, and re-layouts: 19 us -> 6.67 us
    another operation x7 -> x0, local copies, waits for them, and re-layouts: 10.1 us -> none  [the longest x4 6.53 us: sum_by_parts(): return whole[:len(lines)].reshape(shard.shape)]
    all_to_all x4 -> x0, other arithmetic: 8.95 us -> none  [the longest x2 4.48 us: sent_to_all(): return lax.all_to_all(copies, axis, split_axis=0, concat_axis=0, tiled=True)]
    transpose x5 -> x0, local copies, waits for them, and re-layouts: 8.49 us -> none  [the longest x3 5.1 us: in_blocks(): return jnp.moveaxis(shard.reshape(*before, length, -1, *after), dim, 0)]
    ppermute x0 -> x6, waiting for transfers between devices: none -> 8.35 us  [swap(): return lax.ppermute(block, C, [(0, 1), (1, 0)])]
    another operation x9, other arithmetic: 54.1 us -> 48.8 us  [the longest x6 27.1 us: per_device(): lower = jnp.linalg.cholesky(gram)]
  transfers between devices with their start and end apart: 0 -> 6, of which waited for: 0 -> 6; matrix products, arithmetic and copies ran while one was open for 0% -> 0% of each run, Pallas kernels for 0% -> 0%
where the time goes in v1:
time: 279 us; the launch traced here: 278 us
  blocking collectives  145 us (52%)
  other arithmetic  65.1 us (23%)
  starting transfers between devices  33.4 us (12%)
  local copies, waits for them, and re-layouts  12.5 us (4%)
  matrix products  12.3 us (4%)
  waiting for transfers between devices  8.35 us (3%)
    all_to_all x11, blocking collectives, exchange(): return lax.all_to_all(blocks, axes, split_axis=0, concat_axis=0, tiled=True)  145 us
    ppermute x6, starting transfers between devices, swap(): return lax.ppermute(block, C, [(0, 1), (1, 0)])  33.4 us
    another operation x6, other arithmetic, per_device(): lower = jnp.linalg.cholesky(gram)  27.1 us
    another operation x3, other arithmetic, solved(): lax.linalg.triangular_solve(lower, rows, left_side=False, lower=True, tra...  21.7 us
    ppermute x6, waiting for transfers between devices, swap(): return lax.ppermute(block, C, [(0, 1), (1, 0)])  8.35 us
    unnamed x19, local copies, waits for them, and re-layouts  6.67 us
  transfers between devices with their start and end apart: 6, of which 6 were waited for; matrix products, arithmetic and copies ran while one was open for 0% of the time, Pallas kernels for 0%

profile of v1, /device:TPU:1, one launch (start us, length us, event | category | flops | bytes accessed | tf_op | source)
XLA Modules:
  0.0 277.8 jit_solution(15869368906613100296)
XLA Ops:
  6.3 8.8 %collective-permute-start = (f32[1024,128]{1,0:T(8,128)}, f32[1024,128]{1,0:T(8,128)}, u32[]{:S(2)}, u32[]{:S(2)}) collective-permute-start(f32[1024,128]{1,0:T(8,128)} %constant_dynamic-slice_fusion.2), channel_id=1, source_target_pairs={{0,64},{64,0},{1,65},{65,1},{2,66},{66,2},{3,67},{67,3},{4,68},{68... | collective-permute-start | bytes 1572872 | tf_op jit(solution)/shard_map/ppermute | solution.py:16
  18.2 12.3 %all_to_all.55 = f32[4,256,128]{2,1,0:T(8,128)} all-to-all(f32[4,256,128]{2,1,0:T(8,128)S(1)} %bitcast.48), channel_id=1, replica_groups=mesh['gx_0'=4,'gx_1'=2,'gy'=8,'gz'=8] {'gx_0'}, dimensions={0} | all-to-all | bytes 1048576 | tf_op jit(solution)/shard_map/all_to_all | solution.py:20
  31.6 22.6 %all_to_all.56 = f32[64,4,128]{2,1,0:T(4,128)S(1)} all-to-all(f32[64,4,128]{2,1,0:T(4,128)S(1)} %bitcast.54), channel_id=1, replica_groups=mesh['gx_0'=4,'gx_1'=2,'gy'=8,'gz'=8] {'gy','gz'}, dimensions={0} | all-to-all | bytes 262144 | tf_op jit(solution)/shard_map/all_to_all | solution.py:20
  54.3 21.4 %all_to_all.57 = bf16[256,4,128]{2,1,0:T(4,128)(2,1)S(1)} all-to-all(bf16[256,4,128]{2,1,0:T(4,128)(2,1)S(1)} %broadcast_in_dim.19), channel_id=1, replica_groups=mesh['gx_0'=4,'gx_1'=2,'gy'=8,'gz'=8] {'gx_0','gy','gz'}, dimensions={0} | all-to-all | bytes 524288 | tf_op jit(solution)/shard_map/all_to_all | solution.py:20
  75.7 6.2 %collective-permute-start.1 = (bf16[1024,128]{1,0:T(8,128)(2,1)S(1)}, bf16[1024,128]{1,0:T(8,128)(2,1)}, u32[]{:S(2)}, u32[]{:S(2)}) collective-permute-start(bf16[1024,128]{1,0:T(8,128)(2,1)S(1)} %bitcast.50), channel_id=1, source_target_pairs={{0,64},{64,0},{1,65},{65,1},{2,66},{66,2},{3,67},{67,3},{4,68},{68... | collective-permute-start | bytes 786440 | tf_op jit(solution)/shard_map/ppermute | solution.py:16
  86.7 2.3 collective-permute-start.2
  90.6 12.3 %all_to_all.58 = f32[4,256,128]{1,2,0:T(8,128)} all-to-all(f32[4,256,128]{1,2,0:T(8,128)S(1)} %bitcast.49), channel_id=1, replica_groups=mesh['gx_0'=4,'gx_1'=2,'gy'=8,'gz'=8] {'gx_0'}, dimensions={0} | all-to-all | bytes 1048576 | tf_op jit(solution)/shard_map/all_to_all | solution.py:20
  105.6 16.0 %all_to_all.59 = f32[64,4,128]{2,1,0:T(4,128)} all-to-all(f32[64,4,128]{2,1,0:T(4,128)S(1)} %bitcast.53), channel_id=1, replica_groups=mesh['gx_0'=4,'gx_1'=2,'gy'=8,'gz'=8] {'gy','gz'}, dimensions={0} | all-to-all | bytes 262144 | tf_op jit(solution)/shard_map/all_to_all | solution.py:20
  122.7 15.4 %all_to_all.60 = f32[64,4,128]{2,1,0:T(4,128)S(1)} all-to-all(f32[64,4,128]{2,1,0:T(4,128)S(1)} %broadcast_in_dim.20), channel_id=1, replica_groups=mesh['gx_0'=4,'gx_1'=2,'gy'=8,'gz'=8] {'gy','gz'}, dimensions={0} | all-to-all | bytes 262144 | tf_op jit(solution)/shard_map/all_to_all | solution.py:20
  138.1 10.0 %all_to_all.61 = f32[4,256,128]{2,1,0:T(8,128)} all-to-all(f32[4,256,128]{2,1,0:T(8,128)S(1)} %broadcast_in_dim.21), channel_id=1, replica_groups=mesh['gx_0'=4,'gx_1'=2,'gy'=8,'gz'=8] {'gx_0'}, dimensions={0} | all-to-all | bytes 1048576 | tf_op jit(solution)/shard_map/all_to_all | solution.py:20
  148.1 6.8 %collective-permute-start.3 = (f32[1024,128]{1,0:T(8,128)}, f32[1024,128]{1,0:T(8,128)}, u32[]{:S(2)}, u32[]{:S(2)}) collective-permute-start(f32[1024,128]{1,0:T(8,128)} %bitcast.7), channel_id=1, source_target_pairs={{0,64},{64,0},{1,65},{65,1},{2,66},{66,2},{3,67},{67,3},{4,68},{68... | collective-permute-start | bytes 1572872 | tf_op jit(solution)/shard_map/ppermute | solution.py:16
  161.0 11.7 %cholesky.44 = f32[128,128]{1,0:T(8,128)S(1)} custom-call(f32[128,128]{1,0:T(8,128)S(1)} %fusion.10), custom_call_target="Cholesky" | custom-call | tf_op jit(solution)/shard_map/jit(cholesky)/cholesky | solution.py:90
  174.0 9.8 %custom-call.8 = f32[1,128,128]{1,2,0:T(8,128)S(1)} custom-call(f32[1,128,128]{2,1,0:T(8,128)S(1)} %fusion.5), custom_call_target="InvertDiagBlocksLowerTriangular" | custom-call | tf_op jit(solution)/shard_map/triangular_solve | solution.py:69
  183.8 2.2 fusion
  188.9 2.3 collective-permute-start.4
  193.2 7.3 %all_to_all.62 = f32[4,16,128]{2,1,0:T(8,128)} all-to-all(f32[4,16,128]{2,1,0:T(8,128)S(1)} %bitcast.55), channel_id=1, replica_groups=mesh['gx_0'=4,'gx_1'=2,'gy'=8,'gz'=8] {'gx_0'}, dimensions={0} | all-to-all | bytes 65536 | tf_op jit(solution)/shard_map/all_to_all | solution.py:20
  201.3 10.3 %all_to_all.63 = f32[8,16,128]{2,1,0:T(8,128)} all-to-all(f32[8,16,128]{2,1,0:T(8,128)S(1)} %broadcast_in_dim.22), channel_id=1, replica_groups=mesh['gx_0'=4,'gx_1'=2,'gy'=8,'gz'=8] {'gy'}, dimensions={0} | all-to-all | bytes 131072 | tf_op jit(solution)/shard_map/all_to_all | solution.py:20
  212.4 10.3 %all_to_all.64 = f32[8,16,128]{2,1,0:T(8,128)} all-to-all(f32[8,16,128]{2,1,0:T(8,128)S(1)} %broadcast_in_dim.23), channel_id=1, replica_groups=mesh['gx_0'=4,'gx_1'=2,'gy'=8,'gz'=8] {'gz'}, dimensions={0} | all-to-all | bytes 131072 | tf_op jit(solution)/shard_map/all_to_all | solution.py:20
  223.6 7.3 %all_to_all.65 = f32[4,16,128]{2,1,0:T(8,128)} all-to-all(f32[4,16,128]{2,1,0:T(8,128)S(1)} %broadcast_in_dim.24), channel_id=1, replica_groups=mesh['gx_0'=4,'gx_1'=2,'gy'=8,'gz'=8] {'gx_0'}, dimensions={0} | all-to-all | bytes 65536 | tf_op jit(solution)/shard_map/all_to_all | solution.py:20
  232.4 7.0 %collective-permute-start.5 = (f32[64,128]{0,1:T(8,128)}, f32[64,128]{0,1:T(8,128)S(1)}, u32[]{:S(2)}, u32[]{:S(2)}) collective-permute-start(f32[64,128]{0,1:T(8,128)} %copy.51), channel_id=1, source_target_pairs={{0,64},{64,0},{1,65},{65,1},{2,66},{66,2},{3,67},{67,3},{4,68},{68... | collective-permute-start | bytes 98312 | tf_op jit(solution)/shard_map/ppermute | solution.py:16
  245.7 13.2 %cholesky.55 = f32[128,128]{1,0:T(8,128)} custom-call(f32[128,128]{1,0:T(8,128)} %fusion.8), custom_call_target="Cholesky" | custom-call | tf_op jit(solution)/shard_map/jit(cholesky)/cholesky | solution.py:95
  260.4 2.1 fusion.11
  264.1 11.3 %custom-call.9 = f32[1,128,128]{1,2,0:T(8,128)} custom-call(f32[1,128,128]{2,1,0:T(8,128)} %get-tuple-element.24), custom_call_target="InvertDiagBlocksLowerTriangular" | custom-call | tf_op jit(solution)/shard_map/triangular_solve | solution.py:69
  275.4 2.4 fusion.6
  (68 shorter events, 45.6 us)
Async XLA Ops:
  0.6 1.9 copy-start
  4.5 1.0 copy-start.1
  6.3 10.6 %collective-permute-start = (f32[1024,128]{1,0:T(8,128)}, f32[1024,128]{1,0:T(8,128)}, u32[]{:S(2)}, u32[]{:S(2)}) collective-permute-start(f32[1024,128]{1,0:T(8,128)} %constant_dynamic-slice_fusion.2), channel_id=1, source_target_pairs={{0,64},{64,0},{1,65},{65,1},{2,66},{66,2},{3,67},{67,3},{4,68},{68... | collective-permute-start | bytes 1572872 | tf_op jit(solution)/shard_map/ppermute | solution.py:16
  75.7 6.2 %copy-start.5 = (bf16[256,4,128]{2,1,0:T(4,128)(2,1)}, bf16[256,4,128]{2,1,0:T(4,128)(2,1)S(1)}, u32[]{:S(2)}) copy-start(bf16[256,4,128]{2,1,0:T(4,128)(2,1)S(1)} %all_to_all.57) | copy-start | bytes 786436
  75.7 7.5 %collective-permute-start.1 = (bf16[1024,128]{1,0:T(8,128)(2,1)S(1)}, bf16[1024,128]{1,0:T(8,128)(2,1)}, u32[]{:S(2)}, u32[]{:S(2)}) collective-permute-start(bf16[1024,128]{1,0:T(8,128)(2,1)S(1)} %bitcast.50), channel_id=1, source_target_pairs={{0,64},{64,0},{1,65},{65,1},{2,66},{66,2},{3,67},{67,3},{4,68},{68... | collective-permute-start | bytes 786440 | tf_op jit(solution)/shard_map/ppermute | solution.py:16
  84.2 2.2 copy-start.4
  86.7 3.8 %collective-permute-start.2 = (f32[1024,128]{0,1:T(8,128)S(1)}, f32[1024,128]{0,1:T(8,128)S(1)}, u32[]{:S(2)}, u32[]{:S(2)}) collective-permute-start(f32[1024,128]{0,1:T(8,128)S(1)} %constant_dynamic-slice_fusion.1), channel_id=1, source_target_pairs={{0,64},{64,0},{1,65},{65,1},{2,66},{66,2},{3,67},{67,3},{4,68},{68... | collective-permute-start | bytes 1572872 | tf_op jit(solution)/shard_map/ppermute | solution.py:16
  148.1 8.5 %collective-permute-start.3 = (f32[1024,128]{1,0:T(8,128)}, f32[1024,128]{1,0:T(8,128)}, u32[]{:S(2)}, u32[]{:S(2)}) collective-permute-start(f32[1024,128]{1,0:T(8,128)} %bitcast.7), channel_id=1, source_target_pairs={{0,64},{64,0},{1,65},{65,1},{2,66},{66,2},{3,67},{67,3},{4,68},{68... | collective-permute-start | bytes 1572872 | tf_op jit(solution)/shard_map/ppermute | solution.py:16
  157.9 0.8 copy-start.2
  157.9 1.0 copy-start.3
  187.7 0.6 copy-start.8
  188.9 3.5 %collective-permute-start.4 = (f32[64,128]{1,0:T(8,128)}, f32[64,128]{1,0:T(8,128)}, u32[]{:S(2)}, u32[]{:S(2)}) collective-permute-start(f32[64,128]{1,0:T(8,128)} %constant_dynamic-slice_fusion), channel_id=1, source_target_pairs={{0,64},{64,0},{1,65},{65,1},{2,66},{66,2},{3,67},{67,3},{4,68},{68... | collective-permute-start | bytes 98312 | tf_op jit(solution)/shard_map/ppermute | solution.py:16
  232.4 7.9 %collective-permute-start.5 = (f32[64,128]{0,1:T(8,128)}, f32[64,128]{0,1:T(8,128)S(1)}, u32[]{:S(2)}, u32[]{:S(2)}) collective-permute-start(f32[64,128]{0,1:T(8,128)} %copy.51), channel_id=1, source_target_pairs={{0,64},{64,0},{1,65},{65,1},{2,66},{66,2},{3,67},{67,3},{4,68},{68... | collective-permute-start | bytes 98312 | tf_op jit(solution)/shard_map/ppermute | solution.py:16
  241.2 0.6 copy-start.6
  241.2 0.6 copy-start.7

commit v2 on v1

v2 whole, which is shorter than its diff:
```python
import functools
import math

import jax
import jax.numpy as jnp
from jax import lax
from jax.experimental import pallas as pl
from jax.experimental.pallas import tpu as pltpu
from jax.sharding import Mesh
from jax.sharding import PartitionSpec as P

X, C, Z, Y = "gx_0", "gx_1", "gy", "gz"
EVERY = (X, C, Z, Y)
F32, BF16 = jnp.float32, jnp.bfloat16

LANES, SUBLANES, BLOCK = 128, 8, 32


def full(value):
    return jnp.broadcast_to(value, (SUBLANES, LANES))


def reciprocal(value):
    guess = pltpu.reciprocal(value, approx=True)
    guess = guess * (2.0 - value * guess)
    return guess * (2.0 - value * guess)


def inverse_root(value):
    guess = lax.rsqrt(value)
    return guess * (1.5 - 0.5 * value * guess * guess)


def three_terms(value):
    high = value.astype(BF16)
    rest = value - high.astype(F32)
    middle = rest.astype(BF16)
    return high, middle, (rest - middle.astype(F32)).astype(BF16)


def bf16_dot(left, right, dims):
    return lax.dot_general(left, right, (dims, ((), ())), preferred_element_type=F32)


FIRSTS, LASTS = ((0,), (0,)), ((1,), (1,))


def self_product(value):
    terms = [term.astype(F32) for term in three_terms(value)]
    left = jnp.concatenate([terms[i] for i in (0, 0, 1, 0, 2, 1)], 0).astype(BF16)
    right = jnp.concatenate([terms[i] for i in (0, 1, 0, 2, 0, 1)], 0).astype(BF16)
    return bf16_dot(left, right, FIRSTS)


def eliminated(rows, start, lane, sub):
    groups = len(rows)
    count = SUBLANES * groups
    columns = [
        [full(rows[v][:, start + m : start + m + 1]) if v >= m // 8 else None for v in range(groups)]
        for m in range(count)
    ]
    inside = (lane >= start) & (lane < start + count)
    solved_rows = [
        jnp.where(inside, jnp.where(lane - start - 8 * v == sub, 1.0, 0.0), rows[v])
        for v in range(groups)
    ]
    upper = list(rows)
    pivots = [None] * groups
    for j in range(count):
        at, s = divmod(j, SUBLANES)
        pivot = full(columns[j][at][s : s + 1, :])
        pivots[at] = pivot if s == 0 else jnp.where(sub == s, pivot, pivots[at])
        if j == count - 1:
            break
        scale = reciprocal(pivot)
        steps = {v: columns[j][v] * scale for v in range(at, groups)}
        steps[at] = jnp.where(sub > s, steps[at], 0.0)
        for m in range(j + 1, count):
            entry = full(columns[j][m // 8][m % 8 : m % 8 + 1, :])
            for v in range(m // 8, groups):
                columns[m][v] = columns[m][v] - steps[v] * entry
        for held in (solved_rows, upper):
            row = full(held[at][s : s + 1, :])
            for v in range(at, groups):
                held[v] = held[v] - steps[v] * row
    for v in range(groups):
        root = inverse_root(pivots[v])
        solved_rows[v] = solved_rows[v] * root
        upper[v] = jnp.where(lane >= start + 8 * v + sub, upper[v] * root, 0.0)
    return solved_rows, upper, inside


def factored(gram):
    lane = lax.broadcasted_iota(jnp.int32, (SUBLANES, LANES), 1)
    sub = lax.broadcasted_iota(jnp.int32, (SUBLANES, LANES), 0)
    total, groups = gram.shape[0] // SUBLANES, BLOCK // SUBLANES
    left = [gram[8 * v : 8 * v + 8, :] for v in range(total)]
    inverse, factor = [], []
    for k in range(0, total, groups):
        rows, upper, inside = eliminated(left[k : k + groups], SUBLANES * k, lane, sub)
        factor += upper
        inverse += [jnp.where(lane <= 8 * (k + v) + sub, rows[v], 0.0) for v in range(groups)]
        if k + groups < total:
            update = self_product(jnp.concatenate(rows, 0))
            for v in range(k + groups, total):
                left[v] = jnp.where(inside, 0.0, left[v]) - update[8 * v : 8 * v + 8, :]
    return jnp.concatenate(inverse, 0), jnp.concatenate(factor, 0)


def times_transposed(rows, matrix):
    high, middle, low = three_terms(matrix)
    left = jnp.concatenate([rows[i] for i in (0, 0, 1, 0, 2, 1)], 1)
    right = jnp.concatenate([high, middle, high, low, high, middle], 1)
    return bf16_dot(left, right, LASTS)


def middle_kernel(
    scales, core, outcomes, weights_mine, weights_other, back_mine, back_other,
    projected, gram_mine, gram_other, panel, copied,
):
    per_unit, per_day, gram_scale, last_scale = scales
    fetch = pltpu.make_async_copy(outcomes, panel, copied)
    fetch.start()
    half = back_mine.shape[0]
    gram = jnp.zeros((LANES, LANES), F32)
    terms = []
    for weights, back in ((weights_mine, back_mine), (weights_other, back_other)):
        split = three_terms(back[...])
        terms.append(split)
        product = bf16_dot(weights[...], jnp.concatenate(split, 1), FIRSTS)
        for i in range(3):
            gram += product[:, LANES * i : LANES * (i + 1)]
    inverse, _ = factored(gram * gram_scale)
    fresh = [(times_transposed(split, inverse) * per_unit).astype(BF16) for split in terms]
    fetch.wait()
    result = jnp.zeros(projected.shape, F32)
    for i, part in enumerate(fresh):
        side = core[0] if i == 0 else 1 - core[0]
        days = panel[:, pl.ds(pl.multiple_of(side * half, half), half)]
        result += jnp.dot(days, part, preferred_element_type=F32)
    result = result * per_day
    projected[...] = result
    high, middle, low = three_terms(result)
    product = bf16_dot(high, jnp.concatenate([high, middle, low], 1), FIRSTS)
    cross = product[:, LANES : 2 * LANES] + product[:, 2 * LANES :]
    total = product[:, :LANES] + bf16_dot(middle, middle, FIRSTS) + cross + cross.T
    total = total * last_scale
    first = core[0] == 0
    top, bottom = total[: LANES // 2], total[LANES // 2 :]
    gram_mine[...] = jnp.where(first, top, bottom)
    gram_other[...] = jnp.where(first, bottom, top)


def last_kernel(core, gram_mine, gram_other, projected, basis, factor):
    first = core[0] == 0
    mine, other = gram_mine[...], gram_other[...]
    gram = jnp.concatenate([jnp.where(first, mine, other), jnp.where(first, other, mine)], 0)
    inverse, upper = factored(gram)
    factor[...] = upper
    basis[...] = times_transposed(three_terms(projected[...]), inverse)


def specs(*spaces):
    return [pl.BlockSpec(memory_space=space) for space in spaces]


def shapes(*dims):
    return [jax.ShapeDtypeStruct(dim, F32) for dim in dims]


VMEM, SMEM, ANY = pltpu.VMEM, pltpu.SMEM, pl.ANY


def middle_stage(core, outcomes, weights, back, scales):
    rows, rank = outcomes.shape[0], back[0].shape[1]
    return pl.pallas_call(
        functools.partial(middle_kernel, scales),
        out_shape=shapes((rows, rank), (rank // 2, rank), (rank // 2, rank)),
        in_specs=specs(SMEM, ANY, VMEM, VMEM, VMEM, VMEM),
        out_specs=specs(VMEM, VMEM, VMEM),
        scratch_shapes=[pltpu.VMEM(outcomes.shape, BF16), pltpu.SemaphoreType.DMA],
        compiler_params=pltpu.CompilerParams(vmem_limit_bytes=32 << 20),
        name="middle_stage",
    )(core, outcomes, *weights, *back)


def last_stage(core, gram, projected):
    rank = projected.shape[1]
    return pl.pallas_call(
        last_kernel,
        out_shape=shapes(projected.shape, (rank, rank)),
        in_specs=specs(SMEM, VMEM, VMEM, VMEM),
        out_specs=specs(VMEM, VMEM),
        compiler_params=pltpu.CompilerParams(vmem_limit_bytes=16 << 20),
        name="last_stage",
    )(core, *gram, projected)


def swap(block):
    return lax.ppermute(block, C, [(0, 1), (1, 0)])


def exchange(blocks, axes):
    return lax.all_to_all(blocks, axes, split_axis=0, concat_axis=0, tiled=True)


def to_all(block, axes):
    copies = jnp.broadcast_to(block, (lax.axis_size(axes), *block.shape))
    return exchange(copies, axes)


def own_half(whole):
    half = whole.shape[0] // 2
    core = lax.axis_index(C)
    mine = lax.dynamic_slice_in_dim(whole, core * half, half, 0)
    other = lax.dynamic_slice_in_dim(whole, (1 - core) * half, half, 0)
    return mine + swap(other)


def scattered_sum(part, axes):
    blocks = part.reshape(lax.axis_size(axes), -1, part.shape[-1])
    return exchange(blocks, axes).sum(axis=0)


def gathered(own, axes):
    return to_all(own, axes).reshape(-1, own.shape[-1])


def row_sums(part):
    mine = own_half(part)
    mine = scattered_sum(mine, X)
    return scattered_sum(mine, (Z, Y))


def gram_sum(mine, other):
    mine = scattered_sum(mine + swap(other), X)
    mine = to_all(mine, Z).sum(axis=0)
    mine = to_all(mine, Y).sum(axis=0)
    mine = gathered(mine, X)
    return mine, swap(mine)


def transposed_dot(rows, columns):
    return lax.dot_general(rows, columns, (FIRSTS, ((), ())), preferred_element_type=F32)


def per_device(outcomes, sketch):
    rows_here, day_count = outcomes.shape
    rank = sketch.shape[1]
    unit_count = rows_here * lax.axis_size(EVERY)
    per_unit, per_day = 1 / math.sqrt(unit_count), 1 / math.sqrt(day_count)
    core = lax.axis_index(C).astype(jnp.int32).reshape(1)

    own = row_sums(transposed_dot(outcomes, sketch))
    mine = gathered((own * per_unit).astype(BF16), (X, Z, Y))
    other = swap(mine)
    first = lax.axis_index(C) == 0
    weights = jnp.concatenate([jnp.where(first, mine, other), jnp.where(first, other, mine)], 0)

    projected = jnp.dot(outcomes, weights, preferred_element_type=F32) * per_day
    high = projected.astype(BF16)
    low = (projected - high.astype(F32)).astype(BF16)
    split = transposed_dot(outcomes, jnp.concatenate([high, low], 1))
    own = row_sums(split[:, :rank] + split[:, rank:])
    back = gathered(gathered(own, (Z, Y)), X)
    scales = (per_unit, per_day, per_day / unit_count, 1 / unit_count)
    projected, *halves = middle_stage(core, outcomes, (mine, other), (back, swap(back)), scales)
    return tuple(last_stage(core, gram_sum(*halves), projected))


def solution(mesh):
    finer = Mesh(
        mesh.devices.reshape(4, 2, mesh.shape["gy"], mesh.shape["gz"]), EVERY
    )
    return jax.shard_map(
        per_device,
        mesh=finer,
        in_specs=(P(EVERY, None), P(EVERY, None)),
        out_specs=(P(EVERY, None), P()),
        check_vma=False,
    )
```

time: 279 us -> 217 us (0.78)
  other arithmetic: 65.1 us -> 7.08 us
  Pallas kernels: 0 us -> 13.6 us
  matrix products: 12.3 us -> 5.11 us
  local copies, waits for them, and re-layouts: 12.5 us -> 5.71 us
    another operation x9 -> x0, other arithmetic: 48.8 us -> none  [the longest x6 27.1 us: per_device(): lower = jnp.linalg.cholesky(gram)]
    pallas_call x0 -> x2, Pallas kernels: none -> 13.6 us  [the longest x1 8.88 us: middle_stage(): pl.pallas_call(functools.partial(middle_kernel, scales), out_shape=shapes...]
    another operation x2 -> x0, matrix products: 4.55 us -> none  [solved(): lax.linalg.triangular_solve(lower, rows, left_side=False, lower=True, tra...]
    unnamed x19 -> x10, local copies, waits for them, and re-layouts: 6.67 us -> 3.64 us
where the time goes in v2:
time: 217 us; the launch traced here: 216 us
  blocking collectives  143 us (66%)
  starting transfers between devices  33.4 us (15%)
  Pallas kernels  13.6 us (6%)
  waiting for transfers between devices  7.86 us (4%)
  other arithmetic  7.08 us (3%)
  local copies, waits for them, and re-layouts  5.71 us (3%)
  matrix products  5.11 us (2%)
    all_to_all x11, blocking collectives, exchange(): return lax.all_to_all(blocks, axes, split_axis=0, concat_axis=0, tiled=True)  143 us
    ppermute x6, starting transfers between devices, swap(): return lax.ppermute(block, C, [(0, 1), (1, 0)])  33.4 us
    pallas_call x1, Pallas kernels, middle_stage(): pl.pallas_call(functools.partial(middle_kernel, scales), out_shape=shapes...  8.88 us
    ppermute x6, waiting for transfers between devices, swap(): return lax.ppermute(block, C, [(0, 1), (1, 0)])  7.86 us
    pallas_call x1, Pallas kernels, last_stage(): pl.pallas_call(last_kernel, out_shape=shapes(projected.shape, (rank, rank...  4.7 us
    reduce_sum x5, other arithmetic, scattered_sum(): return exchange(blocks, axes).sum(axis=0)  4.54 us
  transfers between devices with their start and end apart: 6, of which 6 were waited for; matrix products, arithmetic and copies ran while one was open for 0% of the time, Pallas kernels for 0%

profile of v2, /device:TPU:1, one launch (start us, length us, event | category | flops | bytes accessed | tf_op | source)
XLA Modules:
  0.0 216.4 jit_solution(4740968178395481367)
XLA Ops:
  1.6 2.9 %fusion.9 = f32[2048,128]{1,0:T(8,128)S(1)} fusion(bf16[768,2048]{1,0:T(8,128)(2,1)} %outcomes.1, bf16[768,128]{1,0:T(8,128)(2,1)S(1)} %copy-done), kind=kOutput, calls=%fused_computation.21 | convolution fusion | flops 402653184 | bytes 4390912 | tf_op jit(solution)/shard_map/dot_general | solution.py:244
  6.3 8.9 %collective-permute-start = (f32[1024,128]{1,0:T(8,128)}, f32[1024,128]{1,0:T(8,128)}, u32[]{:S(2)}, u32[]{:S(2)}) collective-permute-start(f32[1024,128]{1,0:T(8,128)} %constant_dynamic-slice_fusion.1), channel_id=1, source_target_pairs={{0,64},{64,0},{1,65},{65,1},{2,66},{66,2},{3,67},{67,3},{4,68},{68... | collective-permute-start | bytes 1572872 | tf_op jit(solution)/shard_map/ppermute | solution.py:200
  15.2 1.9 collective-permute-done
  18.3 12.3 %all_to_all.55 = f32[4,256,128]{2,1,0:T(8,128)} all-to-all(f32[4,256,128]{2,1,0:T(8,128)S(1)} %bitcast.26), channel_id=1, replica_groups=mesh['gx_0'=4,'gx_1'=2,'gy'=8,'gz'=8] {'gx_0'}, dimensions={0} | all-to-all | bytes 1048576 | tf_op jit(solution)/shard_map/all_to_all | solution.py:204
  30.6 1.7 reduce_sum.63
  32.4 22.8 %all_to_all.56 = f32[64,4,128]{2,1,0:T(4,128)S(1)} all-to-all(f32[64,4,128]{2,1,0:T(4,128)} %bitcast.30), channel_id=1, replica_groups=mesh['gx_0'=4,'gx_1'=2,'gy'=8,'gz'=8] {'gy','gz'}, dimensions={0} | all-to-all | bytes 262144 | tf_op jit(solution)/shard_map/all_to_all | solution.py:204
  55.3 22.0 %all_to_all.57 = bf16[256,4,128]{2,1,0:T(4,128)(2,1)} all-to-all(bf16[256,4,128]{2,1,0:T(4,128)(2,1)S(1)} %broadcast_in_dim.18), channel_id=1, replica_groups=mesh['gx_0'=4,'gx_1'=2,'gy'=8,'gz'=8] {'gx_0','gy','gz'}, dimensions={0} | all-to-all | bytes 524288 | tf_op jit(solution)/shard_map/all_to_all | solution.py:204
  77.3 6.4 %collective-permute-start.1 = (bf16[1024,128]{1,0:T(8,128)(2,1)}, bf16[1024,128]{1,0:T(8,128)(2,1)}, u32[]{:S(2)}, u32[]{:S(2)}) collective-permute-start(bf16[1024,128]{1,0:T(8,128)(2,1)} %bitcast.3.weights_mine), channel_id=1, source_target_pairs={{0,64},{64,0},{1,65},{65,1},{2,66},{66,2},{3,67},{67,3},{4,68},{68... | collective-permute-start | bytes 786440 | tf_op jit(solution)/shard_map/ppermute | solution.py:200
  88.8 2.3 %collective-permute-start.2 = (f32[1024,128]{0,1:T(8,128)S(1)}, f32[1024,128]{0,1:T(8,128)S(1)}, u32[]{:S(2)}, u32[]{:S(2)}) collective-permute-start(f32[1024,128]{0,1:T(8,128)S(1)} %constant_dynamic-slice_fusion), channel_id=1, source_target_pairs={{0,64},{64,0},{1,65},{65,1},{2,66},{66,2},{3,67},{67,3},{4,68},{68... | collective-permute-start | bytes 1572872 | tf_op jit(solution)/shard_map/ppermute | solution.py:200
  91.1 1.5 collective-permute-done.2
  92.7 12.3 %all_to_all.58 = f32[4,256,128]{1,2,0:T(8,128)} all-to-all(f32[4,256,128]{1,2,0:T(8,128)S(1)} %bitcast.27), channel_id=1, replica_groups=mesh['gx_0'=4,'gx_1'=2,'gy'=8,'gz'=8] {'gx_0'}, dimensions={0} | all-to-all | bytes 1048576 | tf_op jit(solution)/shard_map/all_to_all | solution.py:204
  105.0 1.7 reduce_sum.65
  107.7 16.1 %all_to_all.59 = f32[64,4,128]{2,1,0:T(4,128)} all-to-all(f32[64,4,128]{2,1,0:T(4,128)S(1)} %bitcast.29), channel_id=1, replica_groups=mesh['gx_0'=4,'gx_1'=2,'gy'=8,'gz'=8] {'gy','gz'}, dimensions={0} | all-to-all | bytes 262144 | tf_op jit(solution)/shard_map/all_to_all | solution.py:204
  124.9 15.3 %all_to_all.60 = f32[64,4,128]{2,1,0:T(4,128)S(1)} all-to-all(f32[64,4,128]{2,1,0:T(4,128)S(1)} %broadcast_in_dim.19), channel_id=1, replica_groups=mesh['gx_0'=4,'gx_1'=2,'gy'=8,'gz'=8] {'gy','gz'}, dimensions={0} | all-to-all | bytes 262144 | tf_op jit(solution)/shard_map/all_to_all | solution.py:204
  140.3 9.3 %all_to_all.61 = f32[4,256,128]{2,1,0:T(8,128)S(1)} all-to-all(f32[4,256,128]{2,1,0:T(8,128)S(1)} %broadcast_in_dim.20), channel_id=1, replica_groups=mesh['gx_0'=4,'gx_1'=2,'gy'=8,'gz'=8] {'gx_0'}, dimensions={0} | all-to-all | bytes 1048576 | tf_op jit(solution)/shard_map/all_to_all | solution.py:204
  149.6 6.8 %collective-permute-start.3 = (f32[1024,128]{1,0:T(8,128)S(1)}, f32[1024,128]{1,0:T(8,128)S(1)}, u32[]{:S(2)}, u32[]{:S(2)}) collective-permute-start(f32[1024,128]{1,0:T(8,128)S(1)} %bitcast.21), channel_id=1, source_target_pairs={{0,64},{64,0},{1,65},{65,1},{2,66},{66,2},{3,67},{67,3},{4,68},{68... | collective-permute-start | bytes 1572872 | tf_op jit(solution)/shard_map/ppermute | solution.py:200
  157.7 8.9 %middle_stage.1 = (f32[768,128]{1,0:T(8,128)S(1)}, f32[64,128]{1,0:T(8,128)S(1)}, f32[64,128]{1,0:T(8,128)S(1)}) custom-call(s32[1]{0:T(128)} %bitcast.core, bf16[768,2048]{1,0:T(8,128)(2,1)S(1)} %copy-done.1, bf16[1024,128]{1,0:T(8,128)(2,1)} %bitcast.3.weights_mine, bf16[1024,128]{1,0:T(8,128)(2,1)} %collective-permute-done.1.weights_other, ...), custom_call_target="tpu_custom_call" | custom-call | tf_op jit(solution)/shard_map/middle_stage/pallas_call | solution.py:176
  167.3 2.3 %collective-permute-start.4 = (f32[64,128]{1,0:T(8,128)S(1)}, f32[64,128]{1,0:T(8,128)S(1)}, u32[]{:S(2)}, u32[]{:S(2)}) collective-permute-start(f32[64,128]{1,0:T(8,128)S(1)} %get-tuple-element.6), channel_id=1, source_target_pairs={{0,64},{64,0},{1,65},{65,1},{2,66},{66,2},{3,67},{67,3},{4,68},{68... | collective-permute-start | bytes 98312 | tf_op jit(solution)/shard_map/ppermute | solution.py:200
  170.4 6.6 %all_to_all.62 = f32[4,16,128]{2,1,0:T(8,128)S(1)} all-to-all(f32[4,16,128]{2,1,0:T(8,128)S(1)} %bitcast.31), channel_id=1, replica_groups=mesh['gx_0'=4,'gx_1'=2,'gy'=8,'gz'=8] {'gx_0'}, dimensions={0} | all-to-all | bytes 65536 | tf_op jit(solution)/shard_map/all_to_all | solution.py:204
  177.1 9.6 %all_to_all.63 = f32[8,16,128]{2,1,0:T(8,128)S(1)} all-to-all(f32[8,16,128]{2,1,0:T(8,128)S(1)} %broadcast_in_dim.21), channel_id=1, replica_groups=mesh['gx_0'=4,'gx_1'=2,'gy'=8,'gz'=8] {'gy'}, dimensions={0} | all-to-all | bytes 131072 | tf_op jit(solution)/shard_map/all_to_all | solution.py:204
  186.7 9.7 %all_to_all.64 = f32[8,16,128]{2,1,0:T(8,128)S(1)} all-to-all(f32[8,16,128]{2,1,0:T(8,128)S(1)} %broadcast_in_dim.22), channel_id=1, replica_groups=mesh['gx_0'=4,'gx_1'=2,'gy'=8,'gz'=8] {'gz'}, dimensions={0} | all-to-all | bytes 131072 | tf_op jit(solution)/shard_map/all_to_all | solution.py:204
  196.4 6.7 %all_to_all.65 = f32[4,16,128]{2,1,0:T(8,128)S(1)} all-to-all(f32[4,16,128]{2,1,0:T(8,128)S(1)} %broadcast_in_dim.23), channel_id=1, replica_groups=mesh['gx_0'=4,'gx_1'=2,'gy'=8,'gz'=8] {'gx_0'}, dimensions={0} | all-to-all | bytes 65536 | tf_op jit(solution)/shard_map/all_to_all | solution.py:204
  203.1 6.8 %collective-permute-start.5 = (f32[64,128]{1,0:T(8,128)S(1)}, f32[64,128]{1,0:T(8,128)S(1)}, u32[]{:S(2)}, u32[]{:S(2)}) collective-permute-start(f32[64,128]{1,0:T(8,128)S(1)} %bitcast.23), channel_id=1, source_target_pairs={{0,64},{64,0},{1,65},{65,1},{2,66},{66,2},{3,67},{67,3},{4,68},{68... | collective-permute-start | bytes 98312 | tf_op jit(solution)/shard_map/ppermute | solution.py:200
  211.7 4.7 %last_stage.1 = (f32[768,128]{1,0:T(8,128)}, f32[128,128]{1,0:T(8,128)}) custom-call(s32[1]{0:T(128)} %bitcast.core, f32[64,128]{1,0:T(8,128)S(1)} %bitcast.24, f32[64,128]{1,0:T(8,128)S(1)} %collective-permute-done.5.gram_other, f32[768,128]{1,0:T(8,128)S(1)} %copy-done.3), custom_call_target="tpu_custom_call" | custom-call | tf_op jit(solution)/shard_map/last_stage/pallas_call | solution.py:189
  (37 shorter events, 16.0 us)
Async XLA Ops:
  0.6 0.9 copy-start
  4.5 1.0 copy-start.4
  5.5 80.9 %copy-start.1 = (bf16[768,2048]{1,0:T(8,128)(2,1)S(1)}, bf16[768,2048]{1,0:T(8,128)(2,1)}, u32[]{:S(2)}) copy-start(bf16[768,2048]{1,0:T(8,128)(2,1)} %outcomes.1) | copy-start | bytes 9437188
  6.3 10.8 %collective-permute-start = (f32[1024,128]{1,0:T(8,128)}, f32[1024,128]{1,0:T(8,128)}, u32[]{:S(2)}, u32[]{:S(2)}) collective-permute-start(f32[1024,128]{1,0:T(8,128)} %constant_dynamic-slice_fusion.1), channel_id=1, source_target_pairs={{0,64},{64,0},{1,65},{65,1},{2,66},{66,2},{3,67},{67,3},{4,68},{68... | collective-permute-start | bytes 1572872 | tf_op jit(solution)/shard_map/ppermute | solution.py:200
  77.3 7.9 %collective-permute-start.1 = (bf16[1024,128]{1,0:T(8,128)(2,1)}, bf16[1024,128]{1,0:T(8,128)(2,1)}, u32[]{:S(2)}, u32[]{:S(2)}) collective-permute-start(bf16[1024,128]{1,0:T(8,128)(2,1)} %bitcast.3.weights_mine), channel_id=1, source_target_pairs={{0,64},{64,0},{1,65},{65,1},{2,66},{66,2},{3,67},{67,3},{4,68},{68... | collective-permute-start | bytes 786440 | tf_op jit(solution)/shard_map/ppermute | solution.py:200
  88.8 3.8 %collective-permute-start.2 = (f32[1024,128]{0,1:T(8,128)S(1)}, f32[1024,128]{0,1:T(8,128)S(1)}, u32[]{:S(2)}, u32[]{:S(2)}) collective-permute-start(f32[1024,128]{0,1:T(8,128)S(1)} %constant_dynamic-slice_fusion), channel_id=1, source_target_pairs={{0,64},{64,0},{1,65},{65,1},{2,66},{66,2},{3,67},{67,3},{4,68},{68... | collective-permute-start | bytes 1572872 | tf_op jit(solution)/shard_map/ppermute | solution.py:200
  149.6 8.1 %collective-permute-start.3 = (f32[1024,128]{1,0:T(8,128)S(1)}, f32[1024,128]{1,0:T(8,128)S(1)}, u32[]{:S(2)}, u32[]{:S(2)}) collective-permute-start(f32[1024,128]{1,0:T(8,128)S(1)} %bitcast.21), channel_id=1, source_target_pairs={{0,64},{64,0},{1,65},{65,1},{2,66},{66,2},{3,67},{67,3},{4,68},{68... | collective-permute-start | bytes 1572872 | tf_op jit(solution)/shard_map/ppermute | solution.py:200
  166.6 0.7 copy-start.2
  167.3 3.1 %collective-permute-start.4 = (f32[64,128]{1,0:T(8,128)S(1)}, f32[64,128]{1,0:T(8,128)S(1)}, u32[]{:S(2)}, u32[]{:S(2)}) collective-permute-start(f32[64,128]{1,0:T(8,128)S(1)} %get-tuple-element.6), channel_id=1, source_target_pairs={{0,64},{64,0},{1,65},{65,1},{2,66},{66,2},{3,67},{67,3},{4,68},{68... | collective-permute-start | bytes 98312 | tf_op jit(solution)/shard_map/ppermute | solution.py:200
  203.1 7.6 %collective-permute-start.5 = (f32[64,128]{1,0:T(8,128)S(1)}, f32[64,128]{1,0:T(8,128)S(1)}, u32[]{:S(2)}, u32[]{:S(2)}) collective-permute-start(f32[64,128]{1,0:T(8,128)S(1)} %bitcast.23), channel_id=1, source_target_pairs={{0,64},{64,0},{1,65},{65,1},{2,66},{66,2},{3,67},{67,3},{4,68},{68... | collective-permute-start | bytes 98312 | tf_op jit(solution)/shard_map/ppermute | solution.py:200
  210.7 1.0 copy-start.3

commit v3 on v2

--- a/solution.py
+++ b/solution.py
@@ -13,7 +13,7 @@
 EVERY = (X, C, Z, Y)
 F32, BF16 = jnp.float32, jnp.bfloat16
 
-LANES, SUBLANES, BLOCK = 128, 8, 32
+LANES, SUBLANES, BLOCK, CHUNKS = 128, 8, 32, 3
 
 
 def full(value):
@@ -114,14 +114,65 @@
     return bf16_dot(left, right, LASTS)
 
 
+def days_of(panel, side):
+    half = panel.shape[1] // 2
+    return panel[:, pl.ds(pl.multiple_of(side * half, half), half)]
+
+
+def first_kernel(core, outcomes, sketch, mine, other, panel, columns, copied):
+    rows = outcomes.shape[0] // CHUNKS
+    copies = [pltpu.make_async_copy(sketch, columns, copied.at[CHUNKS])]
+    for i in range(CHUNKS):
+        here = pl.ds(i * rows, rows)
+        copies.append(pltpu.make_async_copy(outcomes.at[here], panel.at[here], copied.at[i]))
+    for copy in copies:
+        copy.start()
+    copies[0].wait()
+    for i in range(CHUNKS):
+        copies[i + 1].wait()
+        here = pl.ds(i * rows, rows)
+        for out, side in ((other, 1 - core[0]), (mine, core[0])):
+            product = bf16_dot(days_of(panel.at[here], side), columns[here, :], FIRSTS)
+            out[...] = product if i == 0 else out[...] + product
+
+
+def projection(outcomes, core, weights_mine, weights_other):
+    result = jnp.dot(days_of(outcomes, core[0]), weights_mine, preferred_element_type=F32)
+    return result + jnp.dot(
+        days_of(outcomes, 1 - core[0]), weights_other, preferred_element_type=F32
+    )
+
+
+def back_kernel(
+    per_day, core, outcomes, weights_mine, weights_other, mine, other, panel, copied
+):
+    rows = outcomes.shape[0] // CHUNKS
+    places = [pl.ds(i * rows, rows) for i in range(CHUNKS)]
+    copies = [
+        pltpu.make_async_copy(outcomes.at[here], panel.at[here], copied.at[i])
+        for i, here in enumerate(places)
+    ]
+    for copy in copies:
+        copy.start()
+    for i, here in enumerate(places):
+        copies[i].wait()
+        part = panel.at[here]
+        projected = projection(part, core, weights_mine[...], weights_other[...]) * per_day
+        high, low, _ = three_terms(projected)
+        split = jnp.concatenate([high, low], 1)
+        for out, side in ((other, 1 - core[0]), (mine, core[0])):
+            product = bf16_dot(days_of(part, side), split, FIRSTS)
+            product = product[:, :LANES] + product[:, LANES:]
+            out[...] = product if i == 0 else out[...] + product
+
+
 def middle_kernel(
     scales, core, outcomes, weights_mine, weights_other, back_mine, back_other,
-    projected, gram_mine, gram_other, panel, copied,
+    projected, gram_out, panel, held, copied,
 ):
     per_unit, per_day, gram_scale, last_scale = scales
-    fetch = pltpu.make_async_copy(outcomes, panel, copied)
+    fetch = pltpu.make_async_copy(outcomes, panel, copied.at[0])
     fetch.start()
-    half = back_mine.shape[0]
     gram = jnp.zeros((LANES, LANES), F32)
     terms = []
     for weights, back in ((weights_mine, back_mine), (weights_other, back_other)):
@@ -133,67 +184,115 @@
     inverse, _ = factored(gram * gram_scale)
     fresh = [(times_transposed(split, inverse) * per_unit).astype(BF16) for split in terms]
     fetch.wait()
-    result = jnp.zeros(projected.shape, F32)
-    for i, part in enumerate(fresh):
-        side = core[0] if i == 0 else 1 - core[0]
-        days = panel[:, pl.ds(pl.multiple_of(side * half, half), half)]
-        result += jnp.dot(days, part, preferred_element_type=F32)
-    result = result * per_day
-    projected[...] = result
+    result = projection(panel, core, *fresh) * per_day
+    held[...] = result
+    store = pltpu.make_async_copy(held, projected, copied.at[1])
+    store.start()
     high, middle, low = three_terms(result)
     product = bf16_dot(high, jnp.concatenate([high, middle, low], 1), FIRSTS)
     cross = product[:, LANES : 2 * LANES] + product[:, 2 * LANES :]
     total = product[:, :LANES] + bf16_dot(middle, middle, FIRSTS) + cross + cross.T
-    total = total * last_scale
-    first = core[0] == 0
-    top, bottom = total[: LANES // 2], total[LANES // 2 :]
-    gram_mine[...] = jnp.where(first, top, bottom)
-    gram_other[...] = jnp.where(first, bottom, top)
-
-
-def last_kernel(core, gram_mine, gram_other, projected, basis, factor):
-    first = core[0] == 0
-    mine, other = gram_mine[...], gram_other[...]
-    gram = jnp.concatenate([jnp.where(first, mine, other), jnp.where(first, other, mine)], 0)
-    inverse, upper = factored(gram)
+    gram_out[...] = total * last_scale
+    store.wait()
+
+
+def last_kernel(gram, projected, basis, factor, held, copied):
+    fetch = pltpu.make_async_copy(projected, held, copied)
+    fetch.start()
+    inverse, upper = factored(gram[...])
     factor[...] = upper
-    basis[...] = times_transposed(three_terms(projected[...]), inverse)
+    fetch.wait()
+    basis[...] = times_transposed(three_terms(held[...]), inverse)
+
+
+def sum_kernel(blocks, total):
+    total[...] = blocks[...].sum(axis=0)
 
 
 def specs(*spaces):
     return [pl.BlockSpec(memory_space=space) for space in spaces]
 
 
+VMEM, SMEM, HBM = pltpu.VMEM, pltpu.SMEM, pltpu.HBM
+
+
 def shapes(*dims):
-    return [jax.ShapeDtypeStruct(dim, F32) for dim in dims]
-
-
-VMEM, SMEM, ANY = pltpu.VMEM, pltpu.SMEM, pl.ANY
+    return [VMEM(dim, F32) for dim in dims]
+
+
+def in_hbm(array):
+    return pltpu.with_memory_space_constraint(array, HBM)
+
+
+def first_stage(core, outcomes, sketch):
+    half = (outcomes.shape[1] // 2, sketch.shape[1])
+    return pl.pallas_call(
+        first_kernel,
+        out_shape=shapes(half, half),
+        in_specs=specs(SMEM, HBM, HBM),
+        out_specs=specs(VMEM, VMEM),
+        scratch_shapes=[
+            pltpu.VMEM(outcomes.shape, BF16),
+            pltpu.VMEM(sketch.shape, BF16),
+            pltpu.SemaphoreType.DMA((CHUNKS + 1,)),
+        ],
+        compiler_params=pltpu.CompilerParams(vmem_limit_bytes=16 << 20),
+        name="first_stage",
+    )(core, in_hbm(outcomes), in_hbm(sketch))
+
+
+def back_stage(core, outcomes, weights, per_day):
+    half = weights[0].shape
+    return pl.pallas_call(
+        functools.partial(back_kernel, per_day),
+        out_shape=shapes(half, half),
+        in_specs=specs(SMEM, HBM, VMEM, VMEM),
+        out_specs=specs(VMEM, VMEM),
+        scratch_shapes=[pltpu.VMEM(outcomes.shape, BF16), pltpu.SemaphoreType.DMA((CHUNKS,))],
+        compiler_params=pltpu.CompilerParams(vmem_limit_bytes=24 << 20),
+        name="back_stage",
+    )(core, in_hbm(outcomes), *weights)
 
 
 def middle_stage(core, outcomes, weights, back, scales):
-    rows, rank = outcomes.shape[0], back[0].shape[1]
+    projected = (outcomes.shape[0], back[0].shape[1])
+    rank = projected[1]
     return pl.pallas_call(
         functools.partial(middle_kernel, scales),
-        out_shape=shapes((rows, rank), (rank // 2, rank), (rank // 2, rank)),
-        in_specs=specs(SMEM, ANY, VMEM, VMEM, VMEM, VMEM),
-        out_specs=specs(VMEM, VMEM, VMEM),
-        scratch_shapes=[pltpu.VMEM(outcomes.shape, BF16), pltpu.SemaphoreType.DMA],
-        compiler_params=pltpu.CompilerParams(vmem_limit_bytes=32 << 20),
+        out_shape=[pltpu.HBM(projected, F32), pltpu.VMEM((rank, rank), F32)],
+        in_specs=specs(SMEM, HBM, VMEM, VMEM, VMEM, VMEM),
+        out_specs=specs(HBM, VMEM),
+        scratch_shapes=[
+            pltpu.VMEM(outcomes.shape, BF16),
+            pltpu.VMEM(projected, F32),
+            pltpu.SemaphoreType.DMA((2,)),
+        ],
+        compiler_params=pltpu.CompilerParams(vmem_limit_bytes=24 << 20),
         name="middle_stage",
-    )(core, outcomes, *weights, *back)
-
-
-def last_stage(core, gram, projected):
+    )(core, in_hbm(outcomes), *weights, *back)
+
+
+def last_stage(gram, projected):
     rank = projected.shape[1]
     return pl.pallas_call(
         last_kernel,
-        out_shape=shapes(projected.shape, (rank, rank)),
-        in_specs=specs(SMEM, VMEM, VMEM, VMEM),
+        out_shape=[jax.ShapeDtypeStruct(dim, F32) for dim in (projected.shape, (rank, rank))],
+        in_specs=specs(VMEM, HBM),
         out_specs=specs(VMEM, VMEM),
+        scratch_shapes=[pltpu.VMEM(projected.shape, F32), pltpu.SemaphoreType.DMA],
         compiler_params=pltpu.CompilerParams(vmem_limit_bytes=16 << 20),
         name="last_stage",
-    )(core, *gram, projected)
+    )(gram, in_hbm(projected))
+
+
+def block_sum(blocks):
+    return pl.pallas_call(
+        sum_kernel,
+        out_shape=pltpu.VMEM(blocks.shape[1:], F32),
+        in_specs=specs(VMEM),
+        out_specs=pl.BlockSpec(memory_space=VMEM),
+        name="block_sum",
+    )(pltpu.with_memory_space_constraint(blocks, VMEM))
 
 
 def swap(block):
@@ -209,14 +308,6 @@
     return exchange(copies, axes)
 
 
-def own_half(whole):
-    half = whole.shape[0] // 2
-    core = lax.axis_index(C)
-    mine = lax.dynamic_slice_in_dim(whole, core * half, half, 0)
-    other = lax.dynamic_slice_in_dim(whole, (1 - core) * half, half, 0)
-    return mine + swap(other)
-
-
 def scattered_sum(part, axes):
     blocks = part.reshape(lax.axis_size(axes), -1, part.shape[-1])
     return exchange(blocks, axes).sum(axis=0)
@@ -226,46 +317,33 @@
     return to_all(own, axes).reshape(-1, own.shape[-1])
 
 
-def row_sums(part):
-    mine = own_half(part)
-    mine = scattered_sum(mine, X)
+def row_sums(mine, other):
+    blocks = (mine + swap(other)).reshape(lax.axis_size(X), -1, mine.shape[-1])
+    mine = block_sum(exchange(blocks, X))
     return scattered_sum(mine, (Z, Y))
 
 
-def gram_sum(mine, other):
-    mine = scattered_sum(mine + swap(other), X)
+def gram_sum(part):
+    mine = scattered_sum(part, (X, C))
     mine = to_all(mine, Z).sum(axis=0)
     mine = to_all(mine, Y).sum(axis=0)
-    mine = gathered(mine, X)
-    return mine, swap(mine)
-
-
-def transposed_dot(rows, columns):
-    return lax.dot_general(rows, columns, (FIRSTS, ((), ())), preferred_element_type=F32)
+    return gathered(mine, (X, C))
 
 
 def per_device(outcomes, sketch):
     rows_here, day_count = outcomes.shape
-    rank = sketch.shape[1]
     unit_count = rows_here * lax.axis_size(EVERY)
     per_unit, per_day = 1 / math.sqrt(unit_count), 1 / math.sqrt(day_count)
     core = lax.axis_index(C).astype(jnp.int32).reshape(1)
 
-    own = row_sums(transposed_dot(outcomes, sketch))
+    own = row_sums(*first_stage(core, outcomes, sketch))
     mine = gathered((own * per_unit).astype(BF16), (X, Z, Y))
-    other = swap(mine)
-    first = lax.axis_index(C) == 0
-    weights = jnp.concatenate([jnp.where(first, mine, other), jnp.where(first, other, mine)], 0)
-
-    projected = jnp.dot(outcomes, weights, preferred_element_type=F32) * per_day
-    high = projected.astype(BF16)
-    low = (projected - high.astype(F32)).astype(BF16)
-    split = transposed_dot(outcomes, jnp.concatenate([high, low], 1))
-    own = row_sums(split[:, :rank] + split[:, rank:])
-    back = gathered(gathered(own, (Z, Y)), X)
+    weights = (mine, swap(mine))
+    own = row_sums(*back_stage(core, outcomes, weights, per_day))
+    mine = gathered(gathered(own, (Z, Y)), X)
     scales = (per_unit, per_day, per_day / unit_count, 1 / unit_count)
-    projected, *halves = middle_stage(core, outcomes, (mine, other), (back, swap(back)), scales)
-    return tuple(last_stage(core, gram_sum(*halves), projected))
+    projected, gram = middle_stage(core, outcomes, weights, (mine, swap(mine)), scales)
+    return tuple(last_stage(gram_sum(gram), projected))
 
 
 def solution(mesh):

time: 217 us -> 197 us (0.908)
  starting transfers between devices: 33.4 us -> 24.4 us
  other arithmetic: 7.08 us -> 0.3 us
  Pallas kernels: 13.6 us -> 19.7 us
  local copies, waits for them, and re-layouts: 5.71 us -> 0.15 us
  matrix products: 5.11 us -> 0 us
  waiting for transfers between devices: 7.86 us -> 5.5 us
    ppermute x6 -> x4, starting transfers between devices: 33.4 us -> 24.4 us  [swap(): return lax.ppermute(block, C, [(0, 1), (1, 0)])]
    pallas_call x2 -> x6, Pallas kernels: 13.6 us -> 19.7 us  [the longest x1 7.99 us: middle_stage(): pl.pallas_call(functools.partial(middle_kernel, scales), out_shape=[pltpu...]
    dot_general x3 -> x0, matrix products: 5.11 us -> none  [the longest x2 3.92 us: transposed_dot(): lax.dot_general(rows, columns, (FIRSTS, ((), ())), preferred_element_type...]
    reduce_sum x5 -> x3, other arithmetic: 4.54 us -> 0.17 us  [scattered_sum(): return exchange(blocks, axes).sum(axis=0)]
    unnamed x10 -> x0, local copies, waits for them, and re-layouts: 3.64 us -> none
    all_to_all x11, blocking collectives: 143 us -> 145 us  [exchange(): return lax.all_to_all(blocks, axes, split_axis=0, concat_axis=0, tiled=True)]
    ppermute x6 -> x4, waiting for transfers between devices: 7.86 us -> 5.5 us  [swap(): return lax.ppermute(block, C, [(0, 1), (1, 0)])]
  transfers between devices with their start and end apart: 6 -> 4, of which waited for: 6 -> 4; matrix products, arithmetic and copies ran while one was open for 0% -> 0% of each run, Pallas kernels for 0% -> 0%
where the time goes in v3:
time: 197 us; the launch traced here: 196 us
  blocking collectives  145 us (74%)
  starting transfers between devices  24.4 us (12%)
  Pallas kernels  19.7 us (10%)
  waiting for transfers between devices  5.5 us (3%)
    all_to_all x11, blocking collectives, exchange(): return lax.all_to_all(blocks, axes, split_axis=0, concat_axis=0, tiled=True)  145 us
    ppermute x4, starting transfers between devices, swap(): return lax.ppermute(block, C, [(0, 1), (1, 0)])  24.4 us
    pallas_call x1, Pallas kernels, middle_stage(): pl.pallas_call(functools.partial(middle_kernel, scales), out_shape=[pltpu...  7.99 us
    ppermute x4, waiting for transfers between devices, swap(): return lax.ppermute(block, C, [(0, 1), (1, 0)])  5.5 us
    pallas_call x1, Pallas kernels, last_stage(): pl.pallas_call(last_kernel, out_shape=[jax.ShapeDtypeStruct(dim, F32) for...  5.27 us
  transfers between devices with their start and end apart: 4, of which 4 were waited for; matrix products, arithmetic and copies ran while one was open for 0% of the time, Pallas kernels for 0%

profile of v3, /device:TPU:1, one launch (start us, length us, event | category | flops | bytes accessed | tf_op | source)
XLA Modules:
  0.0 196.2 jit_solution(8928873107145849399)
XLA Ops:
  0.6 2.6 %first_stage.1 = (f32[1024,128]{1,0:T(8,128)S(1)}, f32[1024,128]{1,0:T(8,128)S(1)}) custom-call(s32[1]{0:T(128)} %bitcast.core, bf16[768,2048]{1,0:T(8,128)(2,1)} %outcomes.5, bf16[768,128]{1,0:T(8,128)(2,1)} %sketch.1), custom_call_target="tpu_custom_call" | custom-call | tf_op jit(solution)/shard_map/first_stage/pallas_call | solution.py:229
  3.3 8.8 %collective-permute-start = (f32[1024,128]{1,0:T(8,128)S(1)}, f32[1024,128]{1,0:T(8,128)S(1)}, u32[]{:S(2)}, u32[]{:S(2)}) collective-permute-start(f32[1024,128]{1,0:T(8,128)S(1)} %get-tuple-element.9), channel_id=1, source_target_pairs={{0,64},{64,0},{1,65},{65,1},{2,66},{66,2},{3,67},{67,3},{4,68},{68... | collective-permute-start | bytes 1572872 | tf_op jit(solution)/shard_map/ppermute | solution.py:299
  12.1 1.5 collective-permute-done
  13.7 11.6 %all_to_all.55.blocks = f32[4,256,128]{2,1,0:T(8,128)S(1)} all-to-all(f32[4,256,128]{2,1,0:T(8,128)S(1)} %bitcast.19), channel_id=1, replica_groups=mesh['gx_0'=4,'gx_1'=2,'gy'=8,'gz'=8] {'gx_0'}, dimensions={0} | all-to-all | bytes 1048576 | tf_op jit(solution)/shard_map/all_to_all | solution.py:303
  25.3 23.1 %all_to_all.56 = f32[64,4,128]{2,1,0:T(4,128)S(1)} all-to-all(f32[64,4,128]{2,1,0:T(4,128)S(1)} %bitcast.15), channel_id=1, replica_groups=mesh['gx_0'=4,'gx_1'=2,'gy'=8,'gz'=8] {'gy','gz'}, dimensions={0} | all-to-all | bytes 262144 | tf_op jit(solution)/shard_map/all_to_all | solution.py:303
  48.6 21.4 %all_to_all.57 = bf16[256,4,128]{2,1,0:T(4,128)(2,1)S(1)} all-to-all(bf16[256,4,128]{2,1,0:T(4,128)(2,1)S(1)} %broadcast_in_dim.18), channel_id=1, replica_groups=mesh['gx_0'=4,'gx_1'=2,'gy'=8,'gz'=8] {'gx_0','gy','gz'}, dimensions={0} | all-to-all | bytes 524288 | tf_op jit(solution)/shard_map/all_to_all | solution.py:303
  70.0 6.2 %collective-permute-start.1 = (bf16[1024,128]{1,0:T(8,128)(2,1)S(1)}, bf16[1024,128]{1,0:T(8,128)(2,1)S(1)}, u32[]{:S(2)}, u32[]{:S(2)}) collective-permute-start(bf16[1024,128]{1,0:T(8,128)(2,1)S(1)} %bitcast.10), channel_id=1, source_target_pairs={{0,64},{64,0},{1,65},{65,1},{2,66},{66,2},{3,67},{67,3},{4,68},{68... | collective-permute-start | bytes 786440 | tf_op jit(solution)/shard_map/ppermute | solution.py:299
  76.2 1.1 collective-permute-done.1.weights_other
  77.3 3.8 %back_stage.1 = (f32[1024,128]{1,0:T(8,128)S(1)}, f32[1024,128]{1,0:T(8,128)S(1)}) custom-call(s32[1]{0:T(128)} %bitcast.core, bf16[768,2048]{1,0:T(8,128)(2,1)} %outcomes.5, bf16[1024,128]{1,0:T(8,128)(2,1)S(1)} %bitcast.11, bf16[1024,128]{1,0:T(8,128)(2,1)S(1)} %collective-permute-done.1.weights_other), custom_call_target="tpu_custom_call" | custom-call | tf_op jit(solution)/shard_map/back_stage/pallas_call | solution.py:246
  81.1 2.3 %collective-permute-start.2 = (f32[1024,128]{1,0:T(8,128)S(1)}, f32[1024,128]{1,0:T(8,128)S(1)}, u32[]{:S(2)}, u32[]{:S(2)}) collective-permute-start(f32[1024,128]{1,0:T(8,128)S(1)} %get-tuple-element.11), channel_id=1, source_target_pairs={{0,64},{64,0},{1,65},{65,1},{2,66},{66,2},{3,67},{67,3},{4,68},{68... | collective-permute-start | bytes 1572872 | tf_op jit(solution)/shard_map/ppermute | solution.py:299
  83.4 1.5 collective-permute-done.2
  85.0 11.1 %all_to_all.58.blocks = f32[4,256,128]{2,1,0:T(8,128)S(1)} all-to-all(f32[4,256,128]{2,1,0:T(8,128)S(1)} %bitcast.20), channel_id=1, replica_groups=mesh['gx_0'=4,'gx_1'=2,'gy'=8,'gz'=8] {'gx_0'}, dimensions={0} | all-to-all | bytes 1048576 | tf_op jit(solution)/shard_map/all_to_all | solution.py:303
  96.1 16.2 %all_to_all.59 = f32[64,4,128]{2,1,0:T(4,128)S(1)} all-to-all(f32[64,4,128]{2,1,0:T(4,128)S(1)} %bitcast.16), channel_id=1, replica_groups=mesh['gx_0'=4,'gx_1'=2,'gy'=8,'gz'=8] {'gy','gz'}, dimensions={0} | all-to-all | bytes 262144 | tf_op jit(solution)/shard_map/all_to_all | solution.py:303
  112.3 0.1 reduce_sum.46
  112.4 15.3 %all_to_all.60 = f32[64,4,128]{2,1,0:T(4,128)S(1)} all-to-all(f32[64,4,128]{2,1,0:T(4,128)S(1)} %broadcast_in_dim.19), channel_id=1, replica_groups=mesh['gx_0'=4,'gx_1'=2,'gy'=8,'gz'=8] {'gy','gz'}, dimensions={0} | all-to-all | bytes 262144 | tf_op jit(solution)/shard_map/all_to_all | solution.py:303
  127.8 9.3 %all_to_all.61 = f32[4,256,128]{2,1,0:T(8,128)S(1)} all-to-all(f32[4,256,128]{2,1,0:T(8,128)S(1)} %broadcast_in_dim.20), channel_id=1, replica_groups=mesh['gx_0'=4,'gx_1'=2,'gy'=8,'gz'=8] {'gx_0'}, dimensions={0} | all-to-all | bytes 1048576 | tf_op jit(solution)/shard_map/all_to_all | solution.py:303
  137.1 7.1 %collective-permute-start.3 = (f32[1024,128]{1,0:T(8,128)S(1)}, f32[1024,128]{1,0:T(8,128)S(1)}, u32[]{:S(2)}, u32[]{:S(2)}) collective-permute-start(f32[1024,128]{1,0:T(8,128)S(1)} %bitcast.13), channel_id=1, source_target_pairs={{0,64},{64,0},{1,65},{65,1},{2,66},{66,2},{3,67},{67,3},{4,68},{68... | collective-permute-start | bytes 1572872 | tf_op jit(solution)/shard_map/ppermute | solution.py:299
  144.3 1.3 collective-permute-done.3.back_other
  145.6 8.0 %middle_stage.1 = (f32[768,128]{1,0:T(8,128)}, f32[128,128]{1,0:T(8,128)S(1)}) custom-call(s32[1]{0:T(128)} %bitcast.core, bf16[768,2048]{1,0:T(8,128)(2,1)} %outcomes.5, bf16[1024,128]{1,0:T(8,128)(2,1)S(1)} %bitcast.12, bf16[1024,128]{1,0:T(8,128)(2,1)S(1)} %collective-permute-done.1.weights_other, f32[1024,128]{1,0:T(8,128)S(1)} %bitcast.14, ...), custom_call_target="tpu_custom_call" | custom-call | tf_op jit(solution)/shard_map/middle_stage/pallas_call | solution.py:260
  153.6 7.6 %all_to_all.62 = f32[8,16,128]{2,1,0:T(8,128)S(1)} all-to-all(f32[8,16,128]{2,1,0:T(8,128)S(1)} %bitcast.18), channel_id=1, replica_groups=mesh['gx_0'=4,'gx_1'=2,'gy'=8,'gz'=8] {'gx_0','gx_1'}, dimensions={0} | all-to-all | bytes 131072 | tf_op jit(solution)/shard_map/all_to_all | solution.py:303
  161.2 9.7 %all_to_all.63 = f32[8,16,128]{2,1,0:T(8,128)S(1)} all-to-all(f32[8,16,128]{2,1,0:T(8,128)S(1)} %broadcast_in_dim.21), channel_id=1, replica_groups=mesh['gx_0'=4,'gx_1'=2,'gy'=8,'gz'=8] {'gy'}, dimensions={0} | all-to-all | bytes 131072 | tf_op jit(solution)/shard_map/all_to_all | solution.py:303
  170.9 9.7 %all_to_all.64 = f32[8,16,128]{2,1,0:T(8,128)S(1)} all-to-all(f32[8,16,128]{2,1,0:T(8,128)S(1)} %broadcast_in_dim.22), channel_id=1, replica_groups=mesh['gx_0'=4,'gx_1'=2,'gy'=8,'gz'=8] {'gz'}, dimensions={0} | all-to-all | bytes 131072 | tf_op jit(solution)/shard_map/all_to_all | solution.py:303
  180.7 10.1 %all_to_all.65 = f32[8,16,128]{2,1,0:T(8,128)S(1)} all-to-all(f32[8,16,128]{2,1,0:T(8,128)S(1)} %broadcast_in_dim.23), channel_id=1, replica_groups=mesh['gx_0'=4,'gx_1'=2,'gy'=8,'gz'=8] {'gx_0','gx_1'}, dimensions={0} | all-to-all | bytes 131072 | tf_op jit(solution)/shard_map/all_to_all | solution.py:303
  190.8 5.3 %last_stage.1 = (f32[768,128]{1,0:T(8,128)}, f32[128,128]{1,0:T(8,128)}) custom-call(f32[128,128]{1,0:T(8,128)S(1)} %bitcast.17, f32[768,128]{1,0:T(8,128)} %get-tuple-element.13.projected), custom_call_target="tpu_custom_call" | custom-call | tf_op jit(solution)/shard_map/last_stage/pallas_call | solution.py:277
  (15 shorter events, 0.4 us)
Async XLA Ops:
  3.3 10.3 %collective-permute-start = (f32[1024,128]{1,0:T(8,128)S(1)}, f32[1024,128]{1,0:T(8,128)S(1)}, u32[]{:S(2)}, u32[]{:S(2)}) collective-permute-start(f32[1024,128]{1,0:T(8,128)S(1)} %get-tuple-element.9), channel_id=1, source_target_pairs={{0,64},{64,0},{1,65},{65,1},{2,66},{66,2},{3,67},{67,3},{4,68},{68... | collective-permute-start | bytes 1572872 | tf_op jit(solution)/shard_map/ppermute | solution.py:299
  70.0 7.4 %collective-permute-start.1 = (bf16[1024,128]{1,0:T(8,128)(2,1)S(1)}, bf16[1024,128]{1,0:T(8,128)(2,1)S(1)}, u32[]{:S(2)}, u32[]{:S(2)}) collective-permute-start(bf16[1024,128]{1,0:T(8,128)(2,1)S(1)} %bitcast.10), channel_id=1, source_target_pairs={{0,64},{64,0},{1,65},{65,1},{2,66},{66,2},{3,67},{67,3},{4,68},{68... | collective-permute-start | bytes 786440 | tf_op jit(solution)/shard_map/ppermute | solution.py:299
  81.1 3.8 %collective-permute-start.2 = (f32[1024,128]{1,0:T(8,128)S(1)}, f32[1024,128]{1,0:T(8,128)S(1)}, u32[]{:S(2)}, u32[]{:S(2)}) collective-permute-start(f32[1024,128]{1,0:T(8,128)S(1)} %get-tuple-element.11), channel_id=1, source_target_pairs={{0,64},{64,0},{1,65},{65,1},{2,66},{66,2},{3,67},{67,3},{4,68},{68... | collective-permute-start | bytes 1572872 | tf_op jit(solution)/shard_map/ppermute | solution.py:299
  137.1 8.5 %collective-permute-start.3 = (f32[1024,128]{1,0:T(8,128)S(1)}, f32[1024,128]{1,0:T(8,128)S(1)}, u32[]{:S(2)}, u32[]{:S(2)}) collective-permute-start(f32[1024,128]{1,0:T(8,128)S(1)} %bitcast.13), channel_id=1, source_target_pairs={{0,64},{64,0},{1,65},{65,1},{2,66},{66,2},{3,67},{67,3},{4,68},{68... | collective-permute-start | bytes 1572872 | tf_op jit(solution)/shard_map/ppermute | solution.py:299
